TPU v7x, 32 devices: a whole 2x2x4 slice. The times are simulated.
32 devices in a mesh: feat: 16 (over z, y, x), rows: 2 (over core).
Axes of the slice: x: 2, y: 2, z: 4, core: 2. Of those that a mesh axis runs over, the one named last changes fastest.
Arguments:
- grads: bfloat16 [16384], P(('rows', 'feat')), may hold values from -6 to 6
- hessians: bfloat16 [16384], P(('rows', 'feat')), may hold values from 0.019897461 to 0.25
- nodes: int32 [16384], P(('rows', 'feat')), may hold values from 0 to 15
- bins: int32 [512, 16384], P('feat', 'rows'), may hold values from 0 to 255
Outputs:
- histogram: float32 [2, 16, 512, 256], P(None, 'rows', 'feat')
- best_gain: float32 [16], P('rows')
All inputs are finite; a program needn't handle non-finite values.
Results may differ from a plain program's by a relative error of at most 0.0003.
Values may be sent and summed in bfloat16 or wider, within the bound.
A program may use at most 64 MiB of HBM per device.

v0:
```python
import jax
import jax.numpy as jnp
from jax import lax
from jax.sharding import PartitionSpec as P

BINS = 256
NODES = 16
reg_lambda = 1.0
block_rows = 512


def split_gain(hist):
    left_g = jnp.cumsum(hist[0], axis=-1)
    left_h = jnp.cumsum(hist[1], axis=-1)
    total_g = left_g[..., -1:]
    total_h = left_h[..., -1:]
    gain = left_g * left_g / (left_h + reg_lambda)
    gain = gain + (total_g - left_g) ** 2 / (total_h - left_h + reg_lambda)
    gain = gain - total_g * total_g / (total_h + reg_lambda)
    return jnp.max(gain, axis=(1, 2))


def make_panel(grads, hessians, nodes):
    node_ids = lax.broadcasted_iota(jnp.int32, (NODES, nodes.shape[0]), 0)
    node_hot = (nodes[None, :] == node_ids).astype(jnp.bfloat16)
    return jnp.concatenate([grads[None, :] * node_hot, hessians[None, :] * node_hot], axis=0)


def add_block(hist, bins_block, panel_block):
    count = panel_block.shape[1]
    bin_ids = lax.broadcasted_iota(jnp.int32, (1, BINS, 1), 1)
    one_hot = (bins_block[:, None, :] == bin_ids).astype(jnp.bfloat16).reshape(-1, count)
    return hist + lax.dot_general(
        panel_block, one_hot, (((1,), (1,)), ((), ())), preferred_element_type=jnp.float32
    )


def accumulate(hist, bins_part, panel_part):
    count = panel_part.shape[1]

    def step(which, carry):
        begin = which * block_rows
        bins_block = lax.dynamic_slice_in_dim(bins_part, begin, block_rows, 1)
        panel_block = lax.dynamic_slice_in_dim(panel_part, begin, block_rows, 1)
        return add_block(carry, bins_block, panel_block)

    return lax.fori_loop(0, count // block_rows, step, hist)


def local(grads, hessians, nodes, bins):
    feat_dev = bins.shape[0]
    empty = jnp.zeros((2 * NODES, feat_dev * BINS), jnp.float32)
    local_panel = make_panel(grads, hessians, nodes)
    hist = accumulate(empty, bins, lax.all_gather(local_panel, "feat", axis=1, tiled=True))
    hist = hist.reshape(2, NODES, feat_dev, BINS)
    share = NODES // lax.axis_size("rows")
    total = lax.psum(hist, "rows")
    mine = lax.dynamic_slice_in_dim(total, lax.axis_index("rows") * share, share, 1)
    best = lax.pmax(split_gain(mine), "feat")
    return (mine, best)


def solution(mesh):
    return jax.shard_map(
        local,
        mesh=mesh,
        in_specs=(P(("rows", "feat")), P(("rows", "feat")), P(("rows", "feat")), P("feat", "rows")),
        out_specs=(P(None, "rows", "feat", None), P("rows")),
        check_vma=False,
    )
```

profile of v0, /device:TPU:0, one launch (start us, length us, event | category | flops | bytes accessed | tf_op | source)
XLA Modules:
  0.0 288.1 jit_solution(18204161635696154360)
XLA Ops:
  7.9 45.3 %all_gather.3 = bf16[32,8192]{1,0:T(8,128)(2,1)S(1)} all-gather(bf16[32,512]{1,0:T(8,128)(2,1)S(1)} %pad_maximum_fusion), channel_id=1, replica_groups=mesh['feat'=16,'rows'=2] {'feat'}, dimensions={1}, use_global_device_ids=true | all-gather | bytes 557056 | tf_op jit(solution)/shard_map/all_gather | solution.py:54
  53.3 155.4 %while.14 = (s32[]{:T(128)}, f32[32,8192]{1,0:T(8,128)S(1)}, bf16[32,8192]{1,0:T(8,128)(2,1)S(1)}, s32[32,8192]{1,0:T(8,128)}, s32[]{:T(128)}, /*index=5*/s32[]{:T(128)}, s32[]{:T(128)}, s32[]{:T(128)}) while((s32[]{:T(128)}, f32[32,8192]{1,0:T(8,128)S(1)}, bf16[32,8192]{1,0:T(8,128)(2,1)S(1)}, s32[32,8192]{1,0:T(8,128)}, ...), condition=%wide.region_1.0_spmd.clone, body=%wide.region_0.0_spmd.clone.sunk | while | flops 273154048 | bytes 10846365 | solution.py:47
  54.2 4.0 %bitcast_compare_fusion.2 = pred[8192,512]{1,0:T(32,128)(4,1)} fusion(s32[8192]{0:T(1024)S(1)} %bitcast.39, s32[32,512]{1,0:T(8,128)S(1)} %constant_dynamic-slice_fusion.5), kind=kLoop, calls=%fused_computation.clone.1 | loop fusion | flops 4194304 | bytes 4292608 | tf_op jit(solution)/shard_map/while/body/eval_jaxpr/eq | solution.py:32
  58.1 4.8 %convolution_add_fusion.2 = f32[32,8192]{1,0:T(8,128)S(1)} fusion(pred[8192,512]{1,0:T(32,128)(4,1)} %bitcast_compare_fusion.2, f32[32,8192]{1,0:T(8,128)S(1)} %get-tuple-element.148, pred[]{:T(512)S(6)} %compare.3, bf16[32,8192]{1,0:T(8,128)(2,1)S(1)} %get-tuple-element.157, s32[]{:T(128)S(6)} %select_n.14), kind=kOutput, calls=%fused_computation.1.clone.1 | convolution fusion | flops 268959744 | bytes 6324229 | tf_op jit(solution)/shard_map/while/body/eval_jaxpr/dot_general | solution.py:33
  63.9 4.0 %bitcast_compare_fusion.2 = pred[8192,512]{1,0:T(32,128)(4,1)} fusion(s32[8192]{0:T(1024)S(1)} %bitcast.39, s32[32,512]{1,0:T(8,128)S(1)} %constant_dynamic-slice_fusion.5), kind=kLoop, calls=%fused_computation.clone.1 | loop fusion | flops 4194304 | bytes 4292608 | tf_op jit(solution)/shard_map/while/body/eval_jaxpr/eq | solution.py:32
  67.9 4.8 %convolution_add_fusion.2 = f32[32,8192]{1,0:T(8,128)S(1)} fusion(pred[8192,512]{1,0:T(32,128)(4,1)} %bitcast_compare_fusion.2, f32[32,8192]{1,0:T(8,128)S(1)} %get-tuple-element.148, pred[]{:T(512)S(6)} %compare.3, bf16[32,8192]{1,0:T(8,128)(2,1)S(1)} %get-tuple-element.157, s32[]{:T(128)S(6)} %select_n.14), kind=kOutput, calls=%fused_computation.1.clone.1 | convolution fusion | flops 268959744 | bytes 6324229 | tf_op jit(solution)/shard_map/while/body/eval_jaxpr/dot_general | solution.py:33
  77.6 4.8 %convolution_add_fusion.2 = f32[32,8192]{1,0:T(8,128)S(1)} fusion(pred[8192,512]{1,0:T(32,128)(4,1)} %bitcast_compare_fusion.2, f32[32,8192]{1,0:T(8,128)S(1)} %get-tuple-element.148, pred[]{:T(512)S(6)} %compare.3, bf16[32,8192]{1,0:T(8,128)(2,1)S(1)} %get-tuple-element.157, s32[]{:T(128)S(6)} %select_n.14), kind=kOutput, calls=%fused_computation.1.clone.1 | convolution fusion | flops 268959744 | bytes 6324229 | tf_op jit(solution)/shard_map/while/body/eval_jaxpr/dot_general | solution.py:33
  87.3 4.8 %convolution_add_fusion.2 = f32[32,8192]{1,0:T(8,128)S(1)} fusion(pred[8192,512]{1,0:T(32,128)(4,1)} %bitcast_compare_fusion.2, f32[32,8192]{1,0:T(8,128)S(1)} %get-tuple-element.148, pred[]{:T(512)S(6)} %compare.3, bf16[32,8192]{1,0:T(8,128)(2,1)S(1)} %get-tuple-element.157, s32[]{:T(128)S(6)} %select_n.14), kind=kOutput, calls=%fused_computation.1.clone.1 | convolution fusion | flops 268959744 | bytes 6324229 | tf_op jit(solution)/shard_map/while/body/eval_jaxpr/dot_general | solution.py:33
  97.0 4.8 %convolution_add_fusion.2 = f32[32,8192]{1,0:T(8,128)S(1)} fusion(pred[8192,512]{1,0:T(32,128)(4,1)} %bitcast_compare_fusion.2, f32[32,8192]{1,0:T(8,128)S(1)} %get-tuple-element.148, pred[]{:T(512)S(6)} %compare.3, bf16[32,8192]{1,0:T(8,128)(2,1)S(1)} %get-tuple-element.157, s32[]{:T(128)S(6)} %select_n.14), kind=kOutput, calls=%fused_computation.1.clone.1 | convolution fusion | flops 268959744 | bytes 6324229 | tf_op jit(solution)/shard_map/while/body/eval_jaxpr/dot_general | solution.py:33
  106.7 4.8 %convolution_add_fusion.2 = f32[32,8192]{1,0:T(8,128)S(1)} fusion(pred[8192,512]{1,0:T(32,128)(4,1)} %bitcast_compare_fusion.2, f32[32,8192]{1,0:T(8,128)S(1)} %get-tuple-element.148, pred[]{:T(512)S(6)} %compare.3, bf16[32,8192]{1,0:T(8,128)(2,1)S(1)} %get-tuple-element.157, s32[]{:T(128)S(6)} %select_n.14), kind=kOutput, calls=%fused_computation.1.clone.1 | convolution fusion | flops 268959744 | bytes 6324229 | tf_op jit(solution)/shard_map/while/body/eval_jaxpr/dot_general | solution.py:33
  116.4 4.8 %convolution_add_fusion.2 = f32[32,8192]{1,0:T(8,128)S(1)} fusion(pred[8192,512]{1,0:T(32,128)(4,1)} %bitcast_compare_fusion.2, f32[32,8192]{1,0:T(8,128)S(1)} %get-tuple-element.148, pred[]{:T(512)S(6)} %compare.3, bf16[32,8192]{1,0:T(8,128)(2,1)S(1)} %get-tuple-element.157, s32[]{:T(128)S(6)} %select_n.14), kind=kOutput, calls=%fused_computation.1.clone.1 | convolution fusion | flops 268959744 | bytes 6324229 | tf_op jit(solution)/shard_map/while/body/eval_jaxpr/dot_general | solution.py:33
  126.1 4.8 %convolution_add_fusion.2 = f32[32,8192]{1,0:T(8,128)S(1)} fusion(pred[8192,512]{1,0:T(32,128)(4,1)} %bitcast_compare_fusion.2, f32[32,8192]{1,0:T(8,128)S(1)} %get-tuple-element.148, pred[]{:T(512)S(6)} %compare.3, bf16[32,8192]{1,0:T(8,128)(2,1)S(1)} %get-tuple-element.157, s32[]{:T(128)S(6)} %select_n.14), kind=kOutput, calls=%fused_computation.1.clone.1 | convolution fusion | flops 268959744 | bytes 6324229 | tf_op jit(solution)/shard_map/while/body/eval_jaxpr/dot_general | solution.py:33
  135.8 4.8 %convolution_add_fusion.2 = f32[32,8192]{1,0:T(8,128)S(1)} fusion(pred[8192,512]{1,0:T(32,128)(4,1)} %bitcast_compare_fusion.2, f32[32,8192]{1,0:T(8,128)S(1)} %get-tuple-element.148, pred[]{:T(512)S(6)} %compare.3, bf16[32,8192]{1,0:T(8,128)(2,1)S(1)} %get-tuple-element.157, s32[]{:T(128)S(6)} %select_n.14), kind=kOutput, calls=%fused_computation.1.clone.1 | convolution fusion | flops 268959744 | bytes 6324229 | tf_op jit(solution)/shard_map/while/body/eval_jaxpr/dot_general | solution.py:33
  145.6 4.8 %convolution_add_fusion.2 = f32[32,8192]{1,0:T(8,128)S(1)} fusion(pred[8192,512]{1,0:T(32,128)(4,1)} %bitcast_compare_fusion.2, f32[32,8192]{1,0:T(8,128)S(1)} %get-tuple-element.148, pred[]{:T(512)S(6)} %compare.3, bf16[32,8192]{1,0:T(8,128)(2,1)S(1)} %get-tuple-element.157, s32[]{:T(128)S(6)} %select_n.14), kind=kOutput, calls=%fused_computation.1.clone.1 | convolution fusion | flops 268959744 | bytes 6324229 | tf_op jit(solution)/shard_map/while/body/eval_jaxpr/dot_general | solution.py:33
  155.3 4.8 %convolution_add_fusion.2 = f32[32,8192]{1,0:T(8,128)S(1)} fusion(pred[8192,512]{1,0:T(32,128)(4,1)} %bitcast_compare_fusion.2, f32[32,8192]{1,0:T(8,128)S(1)} %get-tuple-element.148, pred[]{:T(512)S(6)} %compare.3, bf16[32,8192]{1,0:T(8,128)(2,1)S(1)} %get-tuple-element.157, s32[]{:T(128)S(6)} %select_n.14), kind=kOutput, calls=%fused_computation.1.clone.1 | convolution fusion | flops 268959744 | bytes 6324229 | tf_op jit(solution)/shard_map/while/body/eval_jaxpr/dot_general | solution.py:33
  165.0 4.8 %convolution_add_fusion.2 = f32[32,8192]{1,0:T(8,128)S(1)} fusion(pred[8192,512]{1,0:T(32,128)(4,1)} %bitcast_compare_fusion.2, f32[32,8192]{1,0:T(8,128)S(1)} %get-tuple-element.148, pred[]{:T(512)S(6)} %compare.3, bf16[32,8192]{1,0:T(8,128)(2,1)S(1)} %get-tuple-element.157, s32[]{:T(128)S(6)} %select_n.14), kind=kOutput, calls=%fused_computation.1.clone.1 | convolution fusion | flops 268959744 | bytes 6324229 | tf_op jit(solution)/shard_map/while/body/eval_jaxpr/dot_general | solution.py:33
  174.7 4.8 %convolution_add_fusion.2 = f32[32,8192]{1,0:T(8,128)S(1)} fusion(pred[8192,512]{1,0:T(32,128)(4,1)} %bitcast_compare_fusion.2, f32[32,8192]{1,0:T(8,128)S(1)} %get-tuple-element.148, pred[]{:T(512)S(6)} %compare.3, bf16[32,8192]{1,0:T(8,128)(2,1)S(1)} %get-tuple-element.157, s32[]{:T(128)S(6)} %select_n.14), kind=kOutput, calls=%fused_computation.1.clone.1 | convolution fusion | flops 268959744 | bytes 6324229 | tf_op jit(solution)/shard_map/while/body/eval_jaxpr/dot_general | solution.py:33
  184.4 4.8 %convolution_add_fusion.2 = f32[32,8192]{1,0:T(8,128)S(1)} fusion(pred[8192,512]{1,0:T(32,128)(4,1)} %bitcast_compare_fusion.2, f32[32,8192]{1,0:T(8,128)S(1)} %get-tuple-element.148, pred[]{:T(512)S(6)} %compare.3, bf16[32,8192]{1,0:T(8,128)(2,1)S(1)} %get-tuple-element.157, s32[]{:T(128)S(6)} %select_n.14), kind=kOutput, calls=%fused_computation.1.clone.1 | convolution fusion | flops 268959744 | bytes 6324229 | tf_op jit(solution)/shard_map/while/body/eval_jaxpr/dot_general | solution.py:33
  194.1 4.8 %convolution_add_fusion.2 = f32[32,8192]{1,0:T(8,128)S(1)} fusion(pred[8192,512]{1,0:T(32,128)(4,1)} %bitcast_compare_fusion.2, f32[32,8192]{1,0:T(8,128)S(1)} %get-tuple-element.148, pred[]{:T(512)S(6)} %compare.3, bf16[32,8192]{1,0:T(8,128)(2,1)S(1)} %get-tuple-element.157, s32[]{:T(128)S(6)} %select_n.14), kind=kOutput, calls=%fused_computation.1.clone.1 | convolution fusion | flops 268959744 | bytes 6324229 | tf_op jit(solution)/shard_map/while/body/eval_jaxpr/dot_general | solution.py:33
  203.8 4.8 %convolution_add_fusion.2 = f32[32,8192]{1,0:T(8,128)S(1)} fusion(pred[8192,512]{1,0:T(32,128)(4,1)} %bitcast_compare_fusion.2, f32[32,8192]{1,0:T(8,128)S(1)} %get-tuple-element.148, pred[]{:T(512)S(6)} %compare.3, bf16[32,8192]{1,0:T(8,128)(2,1)S(1)} %get-tuple-element.157, s32[]{:T(128)S(6)} %select_n.14), kind=kOutput, calls=%fused_computation.1.clone.1 | convolution fusion | flops 268959744 | bytes 6324229 | tf_op jit(solution)/shard_map/while/body/eval_jaxpr/dot_general | solution.py:33
  210.0 15.4 %all-reduce.2.cloned.1.call-done = f32[2,16,32,256]{3,2,1,0:T(8,128)} async-done(((f32[2,16,32,256]{3,2,1,0:T(8,128)}), f32[2,16,32,256]{3,2,1,0:T(8,128)}) %all-reduce.2.cloned.1.call-update) | async-done | bytes 1048592 | tf_op jit(solution)/shard_map/psum | solution.py:57
  227.0 4.6 %reduce-window.16 = f32[8,32,2,128]{3,1,2,0:T(8,128)S(1)} reduce-window(f32[8,32,2,128]{3,1,2,0:T(8,128)S(1)} %copy.19, f32[]{:T(128)} %constant.45.clone.1), window={size=1x1x1x128 pad=0_0x0_0x0_0x127_0}, to_apply=%region_5.6 | reduce-window | flops 8323072 | bytes 524292 | tf_op jit(solution)/shard_map/reduce-window.2
  231.6 4.6 %reduce-window.14 = f32[8,32,2,128]{3,1,2,0:T(8,128)S(1)} reduce-window(f32[8,32,2,128]{3,1,2,0:T(8,128)S(1)} %copy.16, f32[]{:T(128)} %constant.45.clone.1), window={size=1x1x1x128 pad=0_0x0_0x0_0x127_0}, to_apply=%region_3.0 | reduce-window | flops 8323072 | bytes 524292 | tf_op jit(solution)/shard_map/reduce-window
  237.9 42.5 %pmax.7 = f32[8]{0:T(128)} all-reduce(f32[8]{0:T(128)S(1)} %subtract_reduce_fusion), channel_id=1, replica_groups=mesh['feat'=16,'rows'=2] {'feat'}, use_global_device_ids=true, to_apply=%region_8.9 | all-reduce | flops 8 | bytes 64 | tf_op jit(solution)/shard_map/pmax | solution.py:59
  (89 shorter events, 75.8 us)
Async XLA Ops:
  7.2 218.3 %all-reduce.2.cloned.1.call-start = ((), (), s32[]{:S(2)}) async-start(), calls=%async_computation | async-start | bytes 2097152 | tf_op jit(solution)/shard_map/psum | solution.py:57
  225.5 54.9 %copy-start = (f32[2,16,32,256]{3,2,1,0:T(8,128)S(1)}, f32[2,16,32,256]{3,2,1,0:T(8,128)}, u32[]{:S(2)}) copy-start(f32[2,16,32,256]{3,2,1,0:T(8,128)} %all-reduce.2.cloned.1.call-done) | copy-start | bytes 3145732
Sparse Core Ops, SparseCore 0:
  210.2 15.2 all-reduce.1
where the time goes:
time: 290 us; the launch traced here: 288 us
  blocking collectives  87.8 us (30%)
  matrix products  76.9 us (27%)
  other arithmetic  74.7 us (26%)
  local copies, waits for them, and re-layouts  18.2 us (6%)
  waiting for transfers between devices  15.4 us (5%)
  between operations  14.2 us (5%)
    dot_general x16, matrix products, add_block(): lax.dot_general(panel_block, one_hot, (((1,), (1,)), ((), ())), preferred...  76.9 us
    eq x16, other arithmetic, add_block(): bins_block[:, None, :] == bin_ids  63.8 us
    all_gather x1, blocking collectives, local(): lax.all_gather(local_panel, 'feat', axis=1, tiled=True)  45.3 us
    pmax x1, blocking collectives, local(): best = lax.pmax(split_gain(mine), 'feat')  42.5 us
    psum x1, waiting for transfers between devices, local(): total = lax.psum(hist, 'rows')  15.4 us
    dynamic_slice x16, local copies, waits for them, and re-layouts, step(): bins_block = lax.dynamic_slice_in_dim(bins_part, begin, block_rows, 1)  13.6 us
    another operation x5, other arithmetic  9.56 us
  transfers between devices with their start and end apart: 1, of which 1 were waited for; matrix products, arithmetic and copies ran while one was open for 0% of the time, Pallas kernels for 0%

commit v1 on v0

--- a/solution.py
+++ b/solution.py
@@ -7,6 +7,19 @@
 NODES = 16
 reg_lambda = 1.0
 block_rows = 512
+
+
+def gather_around(value, axis, dim):
+    ways = lax.axis_size(axis)
+    up = [(d, (d + 1) % ways) for d in range(ways)]
+    down = [(d, (d - 1) % ways) for d in range(ways)]
+    earlier, later = ([value], [value])
+    for _ in range(ways // 2):
+        earlier.append(lax.ppermute(earlier[-1], axis, up))
+    for _ in range((ways - 1) // 2):
+        later.append(lax.ppermute(later[-1], axis, down))
+    line = jnp.concatenate([*earlier[::-1], *later[1:]], axis=dim)
+    return jnp.roll(line, (lax.axis_index(axis) - ways // 2) * value.shape[dim], axis=dim)
 
 
 def split_gain(hist):
@@ -51,7 +64,7 @@
     feat_dev = bins.shape[0]
     empty = jnp.zeros((2 * NODES, feat_dev * BINS), jnp.float32)
     local_panel = make_panel(grads, hessians, nodes)
-    hist = accumulate(empty, bins, lax.all_gather(local_panel, "feat", axis=1, tiled=True))
+    hist = accumulate(empty, bins, gather_around(local_panel, "feat", 1))
     hist = hist.reshape(2, NODES, feat_dev, BINS)
     share = NODES // lax.axis_size("rows")
     total = lax.psum(hist, "rows")

time: 290 us -> 312 us (1.076)
  blocking collectives: 87.8 us -> 42.5 us
  starting transfers between devices: 0.04 us -> 42.5 us
  waiting for transfers between devices: 15.4 us -> 39.9 us
    all_gather x1 -> x0, blocking collectives: 45.3 us -> none  [local(): lax.all_gather(local_panel, 'feat', axis=1, tiled=True)]
    ppermute x0 -> x15, starting transfers between devices: none -> 42.4 us  [the longest x7 39.4 us: gather_around(): later.append(lax.ppermute(later[-1], axis, down))]
    ppermute x0 -> x15, waiting for transfers between devices: none -> 19.2 us  [the longest x8 19.1 us: gather_around(): earlier.append(lax.ppermute(earlier[-1], axis, up))]
    psum x1, waiting for transfers between devices: 15.4 us -> 20.8 us  [local(): total = lax.psum(hist, 'rows')]
  transfers between devices with their start and end apart: 1 -> 16, of which waited for: 1 -> 9; matrix products, arithmetic and copies ran while one was open for 0% -> 0% of each run, Pallas kernels for 0% -> 0%
where the time goes in v1:
time: 312 us; the launch traced here: 310 us
  matrix products  76.9 us (25%)
  other arithmetic  75.1 us (24%)
  starting transfers between devices  42.5 us (14%)
  blocking collectives  42.5 us (14%)
  waiting for transfers between devices  39.9 us (13%)
  local copies, waits for them, and re-layouts  18.4 us (6%)
  between operations  14.4 us (5%)
    dot_general x16, matrix products, add_block(): lax.dot_general(panel_block, one_hot, (((1,), (1,)), ((), ())), preferred...  76.9 us
    eq x16, other arithmetic, add_block(): bins_block[:, None, :] == bin_ids  64.1 us
    pmax x1, blocking collectives, local(): best = lax.pmax(split_gain(mine), 'feat')  42.5 us
    ppermute x7, starting transfers between devices, gather_around(): later.append(lax.ppermute(later[-1], axis, down))  39.4 us
    psum x1, waiting for transfers between devices, local(): total = lax.psum(hist, 'rows')  20.8 us
    ppermute x8, waiting for transfers between devices, gather_around(): earlier.append(lax.ppermute(earlier[-1], axis, up))  19.1 us
    dynamic_slice x16, local copies, waits for them, and re-layouts, step(): bins_block = lax.dynamic_slice_in_dim(bins_part, begin, block_rows, 1)  13.6 us
    another operation x5, other arithmetic  9.58 us
  transfers between devices with their start and end apart: 16, of which 9 were waited for; matrix products, arithmetic and copies ran while one was open for 0% of the time, Pallas kernels for 0%

profile of v1, /device:TPU:0, one launch (start us, length us, event | category | flops | bytes accessed | tf_op | source)
XLA Modules:
  0.0 310.3 jit_solution(6490780945914174538)
XLA Ops:
  11.0 5.9 %collective-permute-done = bf16[32,512]{1,0:T(8,128)(2,1)S(1)} collective-permute-done((bf16[32,512]{1,0:T(8,128)(2,1)S(1)}, bf16[32,512]{1,0:T(8,128)(2,1)S(1)}, u32[]{:S(2)}, u32[]{:S(2)}) %collective-permute-start) | collective-permute-done | bytes 32800 | tf_op jit(solution)/shard_map/ppermute | solution.py:18
  16.8 5.6 %collective-permute-start.8 = (bf16[32,512]{1,0:T(8,128)(2,1)S(1)}, bf16[32,512]{1,0:T(8,128)(2,1)S(1)}, u32[]{:S(2)}, u32[]{:S(2)}) collective-permute-start(bf16[32,512]{1,0:T(8,128)(2,1)S(1)} %pad_maximum_fusion), channel_id=1, source_target_pairs={{0,30},{2,0},{4,2},{6,4},{8,6},{10,8},{12,10},{14,12},{16,14},{18,... | collective-permute-start | bytes 98312 | tf_op jit(solution)/shard_map/ppermute | solution.py:20
  24.4 5.6 %collective-permute-start.9 = (bf16[32,512]{1,0:T(8,128)(2,1)S(1)}, bf16[32,512]{1,0:T(8,128)(2,1)S(1)}, u32[]{:S(2)}, u32[]{:S(2)}) collective-permute-start(bf16[32,512]{1,0:T(8,128)(2,1)S(1)} %collective-permute-done.8), channel_id=1, source_target_pairs={{0,30},{2,0},{4,2},{6,4},{8,6},{10,8},{12,10},{14,12},{16,14},{18,... | collective-permute-start | bytes 98312 | tf_op jit(solution)/shard_map/ppermute | solution.py:20
  31.9 5.6 %collective-permute-start.10 = (bf16[32,512]{1,0:T(8,128)(2,1)S(1)}, bf16[32,512]{1,0:T(8,128)(2,1)S(1)}, u32[]{:S(2)}, u32[]{:S(2)}) collective-permute-start(bf16[32,512]{1,0:T(8,128)(2,1)S(1)} %collective-permute-done.9), channel_id=1, source_target_pairs={{0,30},{2,0},{4,2},{6,4},{8,6},{10,8},{12,10},{14,12},{16,14},{18,... | collective-permute-start | bytes 98312 | tf_op jit(solution)/shard_map/ppermute | solution.py:20
  39.4 5.6 %collective-permute-start.11 = (bf16[32,512]{1,0:T(8,128)(2,1)S(1)}, bf16[32,512]{1,0:T(8,128)(2,1)S(1)}, u32[]{:S(2)}, u32[]{:S(2)}) collective-permute-start(bf16[32,512]{1,0:T(8,128)(2,1)S(1)} %collective-permute-done.10), channel_id=1, source_target_pairs={{0,30},{2,0},{4,2},{6,4},{8,6},{10,8},{12,10},{14,12},{16,14},{18,... | collective-permute-start | bytes 98312 | tf_op jit(solution)/shard_map/ppermute | solution.py:20
  46.9 5.6 %collective-permute-start.12 = (bf16[32,512]{1,0:T(8,128)(2,1)S(1)}, bf16[32,512]{1,0:T(8,128)(2,1)S(1)}, u32[]{:S(2)}, u32[]{:S(2)}) collective-permute-start(bf16[32,512]{1,0:T(8,128)(2,1)S(1)} %collective-permute-done.11), channel_id=1, source_target_pairs={{0,30},{2,0},{4,2},{6,4},{8,6},{10,8},{12,10},{14,12},{16,14},{18,... | collective-permute-start | bytes 98312 | tf_op jit(solution)/shard_map/ppermute | solution.py:20
  54.5 5.6 %collective-permute-start.13 = (bf16[32,512]{1,0:T(8,128)(2,1)S(1)}, bf16[32,512]{1,0:T(8,128)(2,1)S(1)}, u32[]{:S(2)}, u32[]{:S(2)}) collective-permute-start(bf16[32,512]{1,0:T(8,128)(2,1)S(1)} %collective-permute-done.12), channel_id=1, source_target_pairs={{0,30},{2,0},{4,2},{6,4},{8,6},{10,8},{12,10},{14,12},{16,14},{18,... | collective-permute-start | bytes 98312 | tf_op jit(solution)/shard_map/ppermute | solution.py:20
  62.0 5.6 %collective-permute-start.14 = (bf16[32,512]{1,0:T(8,128)(2,1)S(1)}, bf16[32,512]{1,0:T(8,128)(2,1)S(1)}, u32[]{:S(2)}, u32[]{:S(2)}) collective-permute-start(bf16[32,512]{1,0:T(8,128)(2,1)S(1)} %collective-permute-done.13), channel_id=1, source_target_pairs={{0,30},{2,0},{4,2},{6,4},{8,6},{10,8},{12,10},{14,12},{16,14},{18,... | collective-permute-start | bytes 98312 | tf_op jit(solution)/shard_map/ppermute | solution.py:20
  70.0 155.6 %while.14 = (s32[]{:T(128)}, f32[32,8192]{1,0:T(8,128)S(1)}, bf16[32,8192]{1,0:T(8,128)(2,1)S(1)}, s32[32,8192]{1,0:T(8,128)}, s32[]{:T(128)}, /*index=5*/s32[]{:T(128)}, s32[]{:T(128)}, s32[]{:T(128)}) while((s32[]{:T(128)}, f32[32,8192]{1,0:T(8,128)S(1)}, bf16[32,8192]{1,0:T(8,128)(2,1)S(1)}, s32[32,8192]{1,0:T(8,128)}, ...), condition=%wide.region_1.2_spmd.clone, body=%wide.region_0.1_spmd.clone.sunk | while | flops 273154048 | bytes 10846357 | solution.py:60
  84.6 4.8 %convolution_add_fusion.2 = f32[32,8192]{1,0:T(8,128)S(1)} fusion(pred[8192,512]{1,0:T(32,128)(4,1)} %bitcast_compare_fusion.2, f32[32,8192]{1,0:T(8,128)S(1)} %get-tuple-element.148, pred[]{:T(512)S(6)} %compare.4, bf16[32,8192]{1,0:T(8,128)(2,1)S(1)} %get-tuple-element.157, s32[]{:T(128)S(6)} %select_n.29), kind=kOutput, calls=%fused_computation.1.clone.1 | convolution fusion | flops 268959744 | bytes 6324229 | tf_op jit(solution)/shard_map/while/body/eval_jaxpr/dot_general | solution.py:46
  94.3 4.8 %convolution_add_fusion.2 = f32[32,8192]{1,0:T(8,128)S(1)} fusion(pred[8192,512]{1,0:T(32,128)(4,1)} %bitcast_compare_fusion.2, f32[32,8192]{1,0:T(8,128)S(1)} %get-tuple-element.148, pred[]{:T(512)S(6)} %compare.4, bf16[32,8192]{1,0:T(8,128)(2,1)S(1)} %get-tuple-element.157, s32[]{:T(128)S(6)} %select_n.29), kind=kOutput, calls=%fused_computation.1.clone.1 | convolution fusion | flops 268959744 | bytes 6324229 | tf_op jit(solution)/shard_map/while/body/eval_jaxpr/dot_general | solution.py:46
  104.1 4.8 %convolution_add_fusion.2 = f32[32,8192]{1,0:T(8,128)S(1)} fusion(pred[8192,512]{1,0:T(32,128)(4,1)} %bitcast_compare_fusion.2, f32[32,8192]{1,0:T(8,128)S(1)} %get-tuple-element.148, pred[]{:T(512)S(6)} %compare.4, bf16[32,8192]{1,0:T(8,128)(2,1)S(1)} %get-tuple-element.157, s32[]{:T(128)S(6)} %select_n.29), kind=kOutput, calls=%fused_computation.1.clone.1 | convolution fusion | flops 268959744 | bytes 6324229 | tf_op jit(solution)/shard_map/while/body/eval_jaxpr/dot_general | solution.py:46
  113.8 4.8 %convolution_add_fusion.2 = f32[32,8192]{1,0:T(8,128)S(1)} fusion(pred[8192,512]{1,0:T(32,128)(4,1)} %bitcast_compare_fusion.2, f32[32,8192]{1,0:T(8,128)S(1)} %get-tuple-element.148, pred[]{:T(512)S(6)} %compare.4, bf16[32,8192]{1,0:T(8,128)(2,1)S(1)} %get-tuple-element.157, s32[]{:T(128)S(6)} %select_n.29), kind=kOutput, calls=%fused_computation.1.clone.1 | convolution fusion | flops 268959744 | bytes 6324229 | tf_op jit(solution)/shard_map/while/body/eval_jaxpr/dot_general | solution.py:46
  123.5 4.8 %convolution_add_fusion.2 = f32[32,8192]{1,0:T(8,128)S(1)} fusion(pred[8192,512]{1,0:T(32,128)(4,1)} %bitcast_compare_fusion.2, f32[32,8192]{1,0:T(8,128)S(1)} %get-tuple-element.148, pred[]{:T(512)S(6)} %compare.4, bf16[32,8192]{1,0:T(8,128)(2,1)S(1)} %get-tuple-element.157, s32[]{:T(128)S(6)} %select_n.29), kind=kOutput, calls=%fused_computation.1.clone.1 | convolution fusion | flops 268959744 | bytes 6324229 | tf_op jit(solution)/shard_map/while/body/eval_jaxpr/dot_general | solution.py:46
  133.2 4.8 %convolution_add_fusion.2 = f32[32,8192]{1,0:T(8,128)S(1)} fusion(pred[8192,512]{1,0:T(32,128)(4,1)} %bitcast_compare_fusion.2, f32[32,8192]{1,0:T(8,128)S(1)} %get-tuple-element.148, pred[]{:T(512)S(6)} %compare.4, bf16[32,8192]{1,0:T(8,128)(2,1)S(1)} %get-tuple-element.157, s32[]{:T(128)S(6)} %select_n.29), kind=kOutput, calls=%fused_computation.1.clone.1 | convolution fusion | flops 268959744 | bytes 6324229 | tf_op jit(solution)/shard_map/while/body/eval_jaxpr/dot_general | solution.py:46
  143.0 4.8 %convolution_add_fusion.2 = f32[32,8192]{1,0:T(8,128)S(1)} fusion(pred[8192,512]{1,0:T(32,128)(4,1)} %bitcast_compare_fusion.2, f32[32,8192]{1,0:T(8,128)S(1)} %get-tuple-element.148, pred[]{:T(512)S(6)} %compare.4, bf16[32,8192]{1,0:T(8,128)(2,1)S(1)} %get-tuple-element.157, s32[]{:T(128)S(6)} %select_n.29), kind=kOutput, calls=%fused_computation.1.clone.1 | convolution fusion | flops 268959744 | bytes 6324229 | tf_op jit(solution)/shard_map/while/body/eval_jaxpr/dot_general | solution.py:46
  152.7 4.8 %convolution_add_fusion.2 = f32[32,8192]{1,0:T(8,128)S(1)} fusion(pred[8192,512]{1,0:T(32,128)(4,1)} %bitcast_compare_fusion.2, f32[32,8192]{1,0:T(8,128)S(1)} %get-tuple-element.148, pred[]{:T(512)S(6)} %compare.4, bf16[32,8192]{1,0:T(8,128)(2,1)S(1)} %get-tuple-element.157, s32[]{:T(128)S(6)} %select_n.29), kind=kOutput, calls=%fused_computation.1.clone.1 | convolution fusion | flops 268959744 | bytes 6324229 | tf_op jit(solution)/shard_map/while/body/eval_jaxpr/dot_general | solution.py:46
  162.4 4.8 %convolution_add_fusion.2 = f32[32,8192]{1,0:T(8,128)S(1)} fusion(pred[8192,512]{1,0:T(32,128)(4,1)} %bitcast_compare_fusion.2, f32[32,8192]{1,0:T(8,128)S(1)} %get-tuple-element.148, pred[]{:T(512)S(6)} %compare.4, bf16[32,8192]{1,0:T(8,128)(2,1)S(1)} %get-tuple-element.157, s32[]{:T(128)S(6)} %select_n.29), kind=kOutput, calls=%fused_computation.1.clone.1 | convolution fusion | flops 268959744 | bytes 6324229 | tf_op jit(solution)/shard_map/while/body/eval_jaxpr/dot_general | solution.py:46
  172.1 4.8 %convolution_add_fusion.2 = f32[32,8192]{1,0:T(8,128)S(1)} fusion(pred[8192,512]{1,0:T(32,128)(4,1)} %bitcast_compare_fusion.2, f32[32,8192]{1,0:T(8,128)S(1)} %get-tuple-element.148, pred[]{:T(512)S(6)} %compare.4, bf16[32,8192]{1,0:T(8,128)(2,1)S(1)} %get-tuple-element.157, s32[]{:T(128)S(6)} %select_n.29), kind=kOutput, calls=%fused_computation.1.clone.1 | convolution fusion | flops 268959744 | bytes 6324229 | tf_op jit(solution)/shard_map/while/body/eval_jaxpr/dot_general | solution.py:46
  181.9 4.8 %convolution_add_fusion.2 = f32[32,8192]{1,0:T(8,128)S(1)} fusion(pred[8192,512]{1,0:T(32,128)(4,1)} %bitcast_compare_fusion.2, f32[32,8192]{1,0:T(8,128)S(1)} %get-tuple-element.148, pred[]{:T(512)S(6)} %compare.4, bf16[32,8192]{1,0:T(8,128)(2,1)S(1)} %get-tuple-element.157, s32[]{:T(128)S(6)} %select_n.29), kind=kOutput, calls=%fused_computation.1.clone.1 | convolution fusion | flops 268959744 | bytes 6324229 | tf_op jit(solution)/shard_map/while/body/eval_jaxpr/dot_general | solution.py:46
  211.1 4.8 %convolution_add_fusion.2 = f32[32,8192]{1,0:T(8,128)S(1)} fusion(pred[8192,512]{1,0:T(32,128)(4,1)} %bitcast_compare_fusion.2, f32[32,8192]{1,0:T(8,128)S(1)} %get-tuple-element.148, pred[]{:T(512)S(6)} %compare.4, bf16[32,8192]{1,0:T(8,128)(2,1)S(1)} %get-tuple-element.157, s32[]{:T(128)S(6)} %select_n.29), kind=kOutput, calls=%fused_computation.1.clone.1 | convolution fusion | flops 268959744 | bytes 6324229 | tf_op jit(solution)/shard_map/while/body/eval_jaxpr/dot_general | solution.py:46
  220.8 4.8 %convolution_add_fusion.2 = f32[32,8192]{1,0:T(8,128)S(1)} fusion(pred[8192,512]{1,0:T(32,128)(4,1)} %bitcast_compare_fusion.2, f32[32,8192]{1,0:T(8,128)S(1)} %get-tuple-element.148, pred[]{:T(512)S(6)} %compare.4, bf16[32,8192]{1,0:T(8,128)(2,1)S(1)} %get-tuple-element.157, s32[]{:T(128)S(6)} %select_n.29), kind=kOutput, calls=%fused_computation.1.clone.1 | convolution fusion | flops 268959744 | bytes 6324229 | tf_op jit(solution)/shard_map/while/body/eval_jaxpr/dot_general | solution.py:46
  227.0 20.8 %all-reduce.2.cloned.1.call-done = f32[2,16,32,256]{3,2,1,0:T(8,128)} async-done(((f32[2,16,32,256]{3,2,1,0:T(8,128)}), f32[2,16,32,256]{3,2,1,0:T(8,128)}) %all-reduce.2.cloned.1.call-update) | async-done | bytes 1048592 | tf_op jit(solution)/shard_map/psum | solution.py:70
  260.2 42.5 %pmax.7 = f32[8]{0:T(128)} all-reduce(f32[8]{0:T(128)S(1)} %subtract_reduce_fusion), channel_id=1, replica_groups=mesh['feat'=16,'rows'=2] {'feat'}, use_global_device_ids=true, to_apply=%region_8.9 | all-reduce | flops 8 | bytes 64 | tf_op jit(solution)/shard_map/pmax | solution.py:72
  (151 shorter events, 124.3 us)
Async XLA Ops:
  7.2 240.6 %all-reduce.2.cloned.1.call-start = ((), (), s32[]{:S(2)}) async-start(), calls=%async_computation | async-start | bytes 2097152 | tf_op jit(solution)/shard_map/psum | solution.py:70
  7.9 8.9 %collective-permute-start = (bf16[32,512]{1,0:T(8,128)(2,1)S(1)}, bf16[32,512]{1,0:T(8,128)(2,1)S(1)}, u32[]{:S(2)}, u32[]{:S(2)}) collective-permute-start(bf16[32,512]{1,0:T(8,128)(2,1)S(1)} %pad_maximum_fusion), channel_id=1, source_target_pairs={{0,2},{2,4},{4,6},{6,8},{8,10},{10,12},{12,14},{14,16},{16,18},{18... | collective-permute-start | bytes 98312 | tf_op jit(solution)/shard_map/ppermute | solution.py:18
  16.8 7.5 %collective-permute-start.1 = (bf16[32,512]{1,0:T(8,128)(2,1)S(1)}, bf16[32,512]{1,0:T(8,128)(2,1)S(1)}, u32[]{:S(2)}, u32[]{:S(2)}) collective-permute-start(bf16[32,512]{1,0:T(8,128)(2,1)S(1)} %collective-permute-done), channel_id=1, source_target_pairs={{0,2},{2,4},{4,6},{6,8},{8,10},{10,12},{12,14},{14,16},{16,18},{18... | collective-permute-start | bytes 98312 | tf_op jit(solution)/shard_map/ppermute | solution.py:18
  16.8 7.5 %collective-permute-start.8 = (bf16[32,512]{1,0:T(8,128)(2,1)S(1)}, bf16[32,512]{1,0:T(8,128)(2,1)S(1)}, u32[]{:S(2)}, u32[]{:S(2)}) collective-permute-start(bf16[32,512]{1,0:T(8,128)(2,1)S(1)} %pad_maximum_fusion), channel_id=1, source_target_pairs={{0,30},{2,0},{4,2},{6,4},{8,6},{10,8},{12,10},{14,12},{16,14},{18,... | collective-permute-start | bytes 98312 | tf_op jit(solution)/shard_map/ppermute | solution.py:20
  24.4 7.5 %collective-permute-start.2 = (bf16[32,512]{1,0:T(8,128)(2,1)S(1)}, bf16[32,512]{1,0:T(8,128)(2,1)S(1)}, u32[]{:S(2)}, u32[]{:S(2)}) collective-permute-start(bf16[32,512]{1,0:T(8,128)(2,1)S(1)} %collective-permute-done.1), channel_id=1, source_target_pairs={{0,2},{2,4},{4,6},{6,8},{8,10},{10,12},{12,14},{14,16},{16,18},{18... | collective-permute-start | bytes 98312 | tf_op jit(solution)/shard_map/ppermute | solution.py:18
  24.4 7.5 %collective-permute-start.9 = (bf16[32,512]{1,0:T(8,128)(2,1)S(1)}, bf16[32,512]{1,0:T(8,128)(2,1)S(1)}, u32[]{:S(2)}, u32[]{:S(2)}) collective-permute-start(bf16[32,512]{1,0:T(8,128)(2,1)S(1)} %collective-permute-done.8), channel_id=1, source_target_pairs={{0,30},{2,0},{4,2},{6,4},{8,6},{10,8},{12,10},{14,12},{16,14},{18,... | collective-permute-start | bytes 98312 | tf_op jit(solution)/shard_map/ppermute | solution.py:20
  31.9 7.5 %collective-permute-start.3 = (bf16[32,512]{1,0:T(8,128)(2,1)S(1)}, bf16[32,512]{1,0:T(8,128)(2,1)S(1)}, u32[]{:S(2)}, u32[]{:S(2)}) collective-permute-start(bf16[32,512]{1,0:T(8,128)(2,1)S(1)} %collective-permute-done.2), channel_id=1, source_target_pairs={{0,2},{2,4},{4,6},{6,8},{8,10},{10,12},{12,14},{14,16},{16,18},{18... | collective-permute-start | bytes 98312 | tf_op jit(solution)/shard_map/ppermute | solution.py:18
  31.9 7.5 %collective-permute-start.10 = (bf16[32,512]{1,0:T(8,128)(2,1)S(1)}, bf16[32,512]{1,0:T(8,128)(2,1)S(1)}, u32[]{:S(2)}, u32[]{:S(2)}) collective-permute-start(bf16[32,512]{1,0:T(8,128)(2,1)S(1)} %collective-permute-done.9), channel_id=1, source_target_pairs={{0,30},{2,0},{4,2},{6,4},{8,6},{10,8},{12,10},{14,12},{16,14},{18,... | collective-permute-start | bytes 98312 | tf_op jit(solution)/shard_map/ppermute | solution.py:20
  39.4 7.5 %collective-permute-start.4 = (bf16[32,512]{1,0:T(8,128)(2,1)S(1)}, bf16[32,512]{1,0:T(8,128)(2,1)S(1)}, u32[]{:S(2)}, u32[]{:S(2)}) collective-permute-start(bf16[32,512]{1,0:T(8,128)(2,1)S(1)} %collective-permute-done.3), channel_id=1, source_target_pairs={{0,2},{2,4},{4,6},{6,8},{8,10},{10,12},{12,14},{14,16},{16,18},{18... | collective-permute-start | bytes 98312 | tf_op jit(solution)/shard_map/ppermute | solution.py:18
  39.4 7.5 %collective-permute-start.11 = (bf16[32,512]{1,0:T(8,128)(2,1)S(1)}, bf16[32,512]{1,0:T(8,128)(2,1)S(1)}, u32[]{:S(2)}, u32[]{:S(2)}) collective-permute-start(bf16[32,512]{1,0:T(8,128)(2,1)S(1)} %collective-permute-done.10), channel_id=1, source_target_pairs={{0,30},{2,0},{4,2},{6,4},{8,6},{10,8},{12,10},{14,12},{16,14},{18,... | collective-permute-start | bytes 98312 | tf_op jit(solution)/shard_map/ppermute | solution.py:20
  46.9 7.6 %collective-permute-start.5 = (bf16[32,512]{1,0:T(8,128)(2,1)S(1)}, bf16[32,512]{1,0:T(8,128)(2,1)S(1)}, u32[]{:S(2)}, u32[]{:S(2)}) collective-permute-start(bf16[32,512]{1,0:T(8,128)(2,1)S(1)} %collective-permute-done.4), channel_id=1, source_target_pairs={{0,2},{2,4},{4,6},{6,8},{8,10},{10,12},{12,14},{14,16},{16,18},{18... | collective-permute-start | bytes 98312 | tf_op jit(solution)/shard_map/ppermute | solution.py:18
  46.9 7.6 %collective-permute-start.12 = (bf16[32,512]{1,0:T(8,128)(2,1)S(1)}, bf16[32,512]{1,0:T(8,128)(2,1)S(1)}, u32[]{:S(2)}, u32[]{:S(2)}) collective-permute-start(bf16[32,512]{1,0:T(8,128)(2,1)S(1)} %collective-permute-done.11), channel_id=1, source_target_pairs={{0,30},{2,0},{4,2},{6,4},{8,6},{10,8},{12,10},{14,12},{16,14},{18,... | collective-permute-start | bytes 98312 | tf_op jit(solution)/shard_map/ppermute | solution.py:20
  54.5 7.5 %collective-permute-start.6 = (bf16[32,512]{1,0:T(8,128)(2,1)S(1)}, bf16[32,512]{1,0:T(8,128)(2,1)S(1)}, u32[]{:S(2)}, u32[]{:S(2)}) collective-permute-start(bf16[32,512]{1,0:T(8,128)(2,1)S(1)} %collective-permute-done.5), channel_id=1, source_target_pairs={{0,2},{2,4},{4,6},{6,8},{8,10},{10,12},{12,14},{14,16},{16,18},{18... | collective-permute-start | bytes 98312 | tf_op jit(solution)/shard_map/ppermute | solution.py:18
  54.5 7.5 %collective-permute-start.13 = (bf16[32,512]{1,0:T(8,128)(2,1)S(1)}, bf16[32,512]{1,0:T(8,128)(2,1)S(1)}, u32[]{:S(2)}, u32[]{:S(2)}) collective-permute-start(bf16[32,512]{1,0:T(8,128)(2,1)S(1)} %collective-permute-done.12), channel_id=1, source_target_pairs={{0,30},{2,0},{4,2},{6,4},{8,6},{10,8},{12,10},{14,12},{16,14},{18,... | collective-permute-start | bytes 98312 | tf_op jit(solution)/shard_map/ppermute | solution.py:20
  62.0 7.5 %collective-permute-start.7 = (bf16[32,512]{1,0:T(8,128)(2,1)S(1)}, bf16[32,512]{1,0:T(8,128)(2,1)S(1)}, u32[]{:S(2)}, u32[]{:S(2)}) collective-permute-start(bf16[32,512]{1,0:T(8,128)(2,1)S(1)} %collective-permute-done.6), channel_id=1, source_target_pairs={{0,2},{2,4},{4,6},{6,8},{8,10},{10,12},{12,14},{14,16},{16,18},{18... | collective-permute-start | bytes 98312 | tf_op jit(solution)/shard_map/ppermute | solution.py:18
  62.0 7.7 %collective-permute-start.14 = (bf16[32,512]{1,0:T(8,128)(2,1)S(1)}, bf16[32,512]{1,0:T(8,128)(2,1)S(1)}, u32[]{:S(2)}, u32[]{:S(2)}) collective-permute-start(bf16[32,512]{1,0:T(8,128)(2,1)S(1)} %collective-permute-done.13), channel_id=1, source_target_pairs={{0,30},{2,0},{4,2},{6,4},{8,6},{10,8},{12,10},{14,12},{16,14},{18,... | collective-permute-start | bytes 98312 | tf_op jit(solution)/shard_map/ppermute | solution.py:20
  247.8 54.9 %copy-start = (f32[2,16,32,256]{3,2,1,0:T(8,128)S(1)}, f32[2,16,32,256]{3,2,1,0:T(8,128)}, u32[]{:S(2)}) copy-start(f32[2,16,32,256]{3,2,1,0:T(8,128)} %all-reduce.2.cloned.1.call-done) | copy-start | bytes 3145732
Sparse Core Ops, SparseCore 0:
  227.1 20.5 all-reduce.1
